TPU v7x, 128 devices: a whole 4x4x4 slice. The times are simulated.
128 devices in a mesh: section: 4 (over x), tensor: 32 (over y, z, core).
Axes of the slice: x: 4, y: 4, z: 4, core: 2. Of those that a mesh axis runs over, the one named last changes fastest.
Arguments:
- hidden_last: bfloat16 [512, 6656], P(None, 'tensor'), may hold values from -6 to 6
- labels: int32 [512], replicated, may hold values from 0 to 31999
- head_weight: bfloat16 [6656, 32000], P(None, 'tensor'), may hold values from -0.21875 to 0.21875
- layer_inputs: bfloat16 [4, 512, 6656], P('section', None, 'tensor'), may hold values from -6 to 6
- weights: bfloat16 [4, 6656, 6656], P('section', 'tensor'), may hold values from -0.078125 to 0.078125
- row_state: float32 [4, 6656], P('section', 'tensor'), may hold values from 1.173753e-06 to 0.000498845
- col_state: float32 [4, 6656], P('section'), may hold values from 1e-08 to 1e-06
Outputs:
- loss: float32 [], replicated
- input_grads: bfloat16 [4, 512, 6656], P('section', None, 'tensor')
- new_weights: bfloat16 [4, 6656, 6656], P('section', 'tensor')
- new_row_state: float32 [4, 6656], P('section', 'tensor')
- new_col_state: float32 [4, 6656], P('section')
All inputs are finite; a program needn't handle non-finite values.
Results may differ from a plain program's by a relative error of at most 0.007.
Values may be sent and summed in bfloat16 or wider, within the bound.
No kernel may reach another device: no remote copies, remote signals or barrier semaphores. Data moves between devices by JAX's collectives and lax.ppermute only.
A program may use at most 128 MiB of HBM per device.

v0:
```python
import jax
import jax.numpy as jnp
from jax import lax
from jax.sharding import Mesh, PartitionSpec as P

decay_rate = 0.9
learn_rate = 0.3
tiny_term = 1e-30
bf16_largest = 3.3895e38


def from_ring(block, axis):
    size = lax.axis_size(axis)
    return [block] + [
        lax.ppermute(block, axis, [(i, (i - step) % size) for i in range(size)])
        for step in range(1, size)
    ]


def rotated(pieces, index, axis=0):
    count = len(pieces)
    placed = []
    for k in range(count):
        chosen = pieces[k]
        for shift in range(1, count):
            chosen = jnp.where(index == shift, pieces[(k - shift) % count], chosen)
        placed.append(chosen)
    return jnp.stack(placed, axis=axis)


def gathered(block, axis, at=0):
    return rotated(from_ring(block, axis), lax.axis_index(axis), at)


def gathered_tensor(block):
    return gathered(gathered(gathered(block, "z"), "y"), "c", 2).reshape(-1, block.shape[-1])


def summed(x, axis):
    pieces = from_ring(x, axis)
    if len(pieces) == 2:
        return pieces[0] + pieces[1]
    return pieces[0] + pieces[2] + (pieces[1] + pieces[3])


def summed_tensor(x):
    return summed(summed(summed(x, "c"), "z"), "y")


def scattered(blocks, axis):
    size = lax.axis_size(axis)
    index = lax.axis_index(axis)
    total = None
    for step in range(size):
        piece = blocks[step]
        for shift in range(1, size):
            piece = jnp.where(index == shift, blocks[(step + shift) % size], piece)
        if step:
            piece = lax.ppermute(
                piece.astype(jnp.bfloat16), axis, [(i, (i + step) % size) for i in range(size)]
            )
        piece = piece.astype(jnp.float32)
        total = piece if total is None else total + piece
    return total


def body(hidden_last, labels, head_weight, layer_inputs, weights, row_state, col_state):
    section_count = lax.axis_size("x")
    section_index = lax.axis_index("x")
    core = lax.axis_index("c")
    all_rows = labels.shape[0]
    model_width, vocab_local = head_weight.shape
    local_weight = weights[0]
    rows_local = local_weight.shape[0]
    saved_all = layer_inputs[0]
    tensor_index = lax.axis_index(("y", "z", "c"))
    columns = tensor_index * vocab_local + lax.iota(jnp.int32, vocab_local)
    share = all_rows // section_count
    row_start = section_index * share
    entries = float(model_width * model_width)
    hidden_rows = lax.dynamic_slice_in_dim(hidden_last, row_start, share, 0).T
    hidden_all = gathered_tensor(hidden_rows)
    logits = lax.dot_general(
        head_weight, hidden_all, (((0,), (0,)), ((), ())), preferred_element_type=jnp.float32
    )
    exponent = jnp.exp(logits)
    label_hit = lax.dynamic_slice_in_dim(labels, row_start, share, 0)[None, :] == columns[:, None]
    weight_float = local_weight.astype(jnp.float32)
    weight_part = jnp.broadcast_to(jnp.sum(weight_float * weight_float), (share,))
    sums = summed_tensor(
        jnp.stack(
            [
                jnp.sum(exponent, axis=0),
                jnp.sum(jnp.where(label_hit, logits, jnp.zeros_like(logits)), axis=0),
                weight_part,
            ]
        )
    )
    denominator, picked, weight_total = (sums[0], sums[1], sums[2, 0])
    both = jnp.concatenate(
        [jnp.minimum(exponent, bf16_largest).astype(jnp.bfloat16), label_hit.astype(jnp.bfloat16)],
        axis=1,
    )
    product = jnp.dot(head_weight, both, preferred_element_type=jnp.float32)
    part = (product[:, :share] / denominator[None, :] - product[:, share:]) / all_rows
    part = part.reshape(4, 4, 2, rows_local, share)
    part = scattered([part[:, :, 0], part[:, :, 1]], "c")
    part = scattered(part, "y")
    part = scattered(part, "z")
    head_grad = gathered(part.astype(jnp.bfloat16), "x", 1).reshape(rows_local, all_rows)
    loss = summed(jnp.sum(jnp.log(denominator) - picked)[None], "x")[0] / all_rows
    dy = head_grad
    outputs = jnp.zeros((rows_local, all_rows), jnp.bfloat16)
    gradient = jnp.zeros((rows_local, model_width), jnp.float32)
    for step in range(4):
        active = step == section_count - 1 - section_index
        full = lax.all_gather(dy, ("y", "z", "c"), axis=0, tiled=True)
        backward = jnp.dot(local_weight, full, preferred_element_type=jnp.float32)
        input_grad = (dy.astype(jnp.float32) + backward).astype(jnp.bfloat16)
        outputs = jnp.where(active, input_grad, outputs)
        if step < 3:
            dy = lax.ppermute(input_grad, "x", [(i, i - 1) for i in range(1, 4)])
        gradient = lax.cond(
            active,
            lambda g, f: lax.dot_general(
                saved_all, f, (((0,), (1,)), ((), ())), preferred_element_type=jnp.float32
            ),
            lambda g, f: g,
            gradient,
            full,
        )
    squares = gradient * gradient
    row_new = decay_rate * row_state[0] + (1.0 - decay_rate) * jnp.mean(squares + tiny_term, axis=1)
    col_part = jnp.sum(squares + tiny_term, axis=0)
    scaled_part = jnp.sum(squares * (1.0 / row_new)[:, None], axis=0)
    row_part = jnp.broadcast_to(jnp.sum(row_new), (128,))
    payload = jnp.concatenate([col_part, scaled_part, row_part]).reshape(-1, 128)
    payload = summed_tensor(payload).reshape(-1)
    col_sum = payload[:model_width]
    scaled_sum = payload[model_width : 2 * model_width]
    row_total = payload[2 * model_width]
    col_new = decay_rate * col_state[0] + (1.0 - decay_rate) * (col_sum / model_width)
    update_total = row_total * jnp.sum(scaled_sum / col_new)
    factor = (
        learn_rate
        * jnp.sqrt(weight_total / entries)
        / jnp.maximum(1.0, jnp.sqrt(update_total / entries))
    )
    row_scale = factor * jnp.sqrt(row_total / row_new)
    col_scale = 1.0 / jnp.sqrt(col_new)
    new_weight = (weight_float - gradient * row_scale[:, None] * col_scale[None, :]).astype(
        jnp.bfloat16
    )
    return (loss, outputs.T[None], new_weight[None], row_new[None], col_new[None])


def solution(mesh):
    fine = Mesh(mesh.devices.reshape(4, 4, 4, 2), ("x", "y", "z", "c"))
    tensor = ("y", "z", "c")
    return jax.shard_map(
        body,
        mesh=fine,
        in_specs=(
            P(None, tensor),
            P(),
            P(None, tensor),
            P("x", None, tensor),
            P("x", tensor, None),
            P("x", tensor),
            P("x", None),
        ),
        out_specs=(P(), P("x", None, tensor), P("x", tensor, None), P("x", tensor), P("x", None)),
        check_vma=False,
    )
```

profile of v0, /device:TPU:6, one launch (start us, length us, event | category | flops | bytes accessed | tf_op | source)
XLA Modules:
  0.0 411.0 jit_solution(6000275937418690555)
XLA Ops:
  10.1 3.6 collective-permute-start.1
  29.0 3.9 collective-permute-done.4
  42.5 8.4 %exponential_reduce_fusion = (f32[128]{0:T(128)S(1)}, f32[128]{0:T(128)S(1)}, bf16[1000,128]{1,0:T(8,128)(2,1)S(1)}) fusion(s32[1000]{0:T(1024)S(1)} %iota_add_fusion, s32[128]{0:T(128)S(1)} %dynamic_slice.7, bf16[6656,128]{1,0:T(8,128)(2,1)S(1)} %bitcast.251, bf16[6656,1000]{0,1:T(8,128)(2,1)} %param.17), kind=kOutput, calls=%fused_computation.43 | convolution fusion | flops 1704703744 | bytes 15277472 | tf_op jit(solution)/shard_map/dot_general | solution.py:83
  63.6 7.0 %convolution_bitcast_fusion = f32[6656,256]{0,1:T(8,128)S(1)} fusion(bf16[6656,1000]{0,1:T(8,128)(2,1)} %param.17, bf16[1000,128]{1,0:T(8,128)(2,1)S(1)} %compare_convert_fusion, bf16[1000,128]{1,0:T(8,128)(2,1)S(1)} %get-tuple-element.58), kind=kOutput, calls=%fused_computation | convolution fusion | flops 3408896000 | bytes 20639744 | tf_op jit(solution)/shard_map/dot_general | solution.py:104
  72.9 3.6 copy.17
  84.4 8.2 %collective-permute-done.18 = bf16[4,208,128]{2,1,0:T(8,128)(2,1)S(1)} collective-permute-done((bf16[4,208,128]{2,1,0:T(8,128)(2,1)S(1)}, bf16[4,208,128]{2,1,0:T(8,128)(2,1)S(1)}, u32[]{:S(2)}, u32[]{:S(2)}) %collective-permute-start.18) | collective-permute-done | bytes 213024 | tf_op jit(solution)/shard_map/ppermute | solution.py:59
  98.4 3.4 collective-permute-done.22
  111.0 50.0 %all-gather.5.cloned.1.call-done = bf16[6656,512]{1,0:T(8,128)(2,1)} async-done(((bf16[208,512]{1,0:T(8,128)(2,1)}), bf16[6656,512]{1,0:T(8,128)(2,1)}) %all-gather.5.cloned.1.call-update) | async-done | bytes 6815760 | tf_op jit(solution)/shard_map/all_gather | solution.py:117
  161.0 5.4 %fusion.27 = bf16[208,512]{1,0:T(8,128)(2,1)S(1)} fusion(bf16[6656,512]{1,0:T(8,128)(2,1)} %all-gather.5.cloned.1.call-done, bf16[1,208,6656]{2,1,0:T(8,128)(2,1)} %param.19, bf16[208,1,128]{2,0,1:T(8,128)(2,1)S(1)} %get-tuple-element.63, bf16[208,1,128]{2,0,1:T(8,128)(2,1)S(1)} %get-tuple-element.64, bf16[208,1,128]{2,0,1:T(8,128)(2,1)S(1)} %get-tuple-element.65, ...), kind=kOutput, calls=%fused_computation.31 | convolution fusion | flops 1418313728 | bytes 10010624 | tf_op jit(solution)/shard_map/dot_general | solution.py:118
  169.2 4.9 %collective-permute-done.27 = bf16[208,512]{1,0:T(8,128)(2,1)S(1)} collective-permute-done((bf16[208,512]{1,0:T(8,128)(2,1)S(1)}, bf16[208,512]{1,0:T(8,128)(2,1)S(1)}, u32[]{:S(2)}, u32[]{:S(2)}) %collective-permute-start.27) | collective-permute-done | bytes 213024 | tf_op jit(solution)/shard_map/ppermute | solution.py:122
  174.8 50.7 %all-gather.7.cloned.1.call-done = bf16[6656,512]{1,0:T(8,128)(2,1)} async-done(((bf16[208,512]{1,0:T(8,128)(2,1)}), bf16[6656,512]{1,0:T(8,128)(2,1)}) %all-gather.7.cloned.1.call-update) | async-done | bytes 6815760 | tf_op jit(solution)/shard_map/all_gather | solution.py:117
  225.5 4.5 %add_convert_fusion.2 = bf16[208,512]{1,0:T(8,128)(2,1)S(1)} fusion(bf16[208,512]{1,0:T(8,128)(2,1)} %copy-done.12, bf16[6656,512]{1,0:T(8,128)(2,1)} %all-gather.7.cloned.1.call-done, bf16[1,208,6656]{2,1,0:T(8,128)(2,1)S(1)} %copy-done.2), kind=kOutput, calls=%fused_computation.50 | convolution fusion | flops 1417994240 | bytes 10010624 | tf_op jit(solution)/shard_map/dot_general | solution.py:118
  232.9 4.9 %collective-permute-done.28 = bf16[208,512]{1,0:T(8,128)(2,1)S(1)} collective-permute-done((bf16[208,512]{1,0:T(8,128)(2,1)S(1)}, bf16[208,512]{1,0:T(8,128)(2,1)S(1)}, u32[]{:S(2)}, u32[]{:S(2)}) %collective-permute-start.28) | collective-permute-done | bytes 213024 | tf_op jit(solution)/shard_map/ppermute | solution.py:122
  238.5 50.7 %all-gather.9.cloned.1.call-done = bf16[6656,512]{1,0:T(8,128)(2,1)} async-done(((bf16[208,512]{1,0:T(8,128)(2,1)}), bf16[6656,512]{1,0:T(8,128)(2,1)}) %all-gather.9.cloned.1.call-update) | async-done | bytes 6815760 | tf_op jit(solution)/shard_map/all_gather | solution.py:117
  289.2 4.5 %add_convert_fusion.1 = bf16[208,512]{1,0:T(8,128)(2,1)S(1)} fusion(bf16[208,512]{1,0:T(8,128)(2,1)} %copy-done.13, bf16[6656,512]{1,0:T(8,128)(2,1)} %all-gather.9.cloned.1.call-done, bf16[1,208,6656]{2,1,0:T(8,128)(2,1)S(1)} %copy-done.2), kind=kOutput, calls=%fused_computation.49 | convolution fusion | flops 1417994240 | bytes 10010624 | tf_op jit(solution)/shard_map/dot_general | solution.py:118
  296.5 4.9 %collective-permute-done.29 = bf16[208,512]{1,0:T(8,128)(2,1)S(1)} collective-permute-done((bf16[208,512]{1,0:T(8,128)(2,1)S(1)}, bf16[208,512]{1,0:T(8,128)(2,1)S(1)}, u32[]{:S(2)}, u32[]{:S(2)}) %collective-permute-start.29) | collective-permute-done | bytes 213024 | tf_op jit(solution)/shard_map/ppermute | solution.py:122
  302.3 7.9 %conditional.4 = (f32[208,6656]{1,0:T(8,128)}) conditional(s32[]{:T(128)} %convert_element_type.126, () %tuple.32, (bf16[512,208]{1,0:T(8,128)(2,1)S(1)}, bf16[6656,512]{1,0:T(8,128)(2,1)}) %tuple.74), branch_computations={%region_4.5_spmd, %region_5.6_spmd} | conditional | flops 1417674752 | bytes 12566536 | solution.py:123
  302.6 7.7 %fusion.48 = f32[208,6656]{1,0:T(8,128)} fusion(bf16[512,208]{1,0:T(8,128)(2,1)S(1)} %get-tuple-element.28, bf16[6656,512]{1,0:T(8,128)(2,1)} %get-tuple-element.32), kind=kOutput, calls=%fused_computation.109 | convolution fusion | flops 1417674752 | bytes 12566528 | tf_op jit(solution)/shard_map/cond/branch_1_fun/dot_general | solution.py:125
  310.2 42.6 %all-gather.11.cloned.1.call-done = bf16[6656,512]{1,0:T(8,128)(2,1)} async-done(((bf16[208,512]{1,0:T(8,128)(2,1)}), bf16[6656,512]{1,0:T(8,128)(2,1)}) %all-gather.11.cloned.1.call-update) | async-done | bytes 6815760 | tf_op jit(solution)/shard_map/all_gather | solution.py:117
  365.8 8.2 %collective-permute-start.16 = (f32[1]{0:T(128)}, f32[1]{0:T(128)}, u32[]{:S(2)}, u32[]{:S(2)}) collective-permute-start(f32[1]{0:T(128)} %bitcast.19), channel_id=1, source_target_pairs={{0,32},{32,64},{64,96},{96,0},{1,33},{33,65},{65,97},{97,1},{2,34}... | collective-permute-start | bytes 20 | tf_op jit(solution)/shard_map/ppermute | solution.py:15
  374.7 4.6 %collective-permute-done.14 = f32[1]{0:T(128)} collective-permute-done((f32[1]{0:T(128)}, f32[1]{0:T(128)}, u32[]{:S(2)}, u32[]{:S(2)}) %collective-permute-start.14) | collective-permute-done | bytes 36 | tf_op jit(solution)/shard_map/ppermute | solution.py:15
  380.5 3.6 collective-permute-done.15
  389.2 5.2 %fusion.36 = bf16[1,512,208]{1,2,0:T(8,128)(2,1)} fusion(bf16[208,512]{1,0:T(8,128)(2,1)S(1)} %copy-done.11, bf16[208,512]{1,0:T(8,128)(2,1)S(1)} %copy-done.21, bf16[208,512]{1,0:T(8,128)(2,1)S(1)} %copy-done.19, bf16[208,512]{1,0:T(8,128)(2,1)S(1)} %copy-done.17, pred[]{:T(512)S(6)} %eq.50, pred[]{:T(512)S(6)} %eq.49, pred[]{:T(512)S(6)} %eq.48, ...), kind=kOutput, calls=%fused_computation.56 | convolution fusion | flops 1418420224 | bytes 10649604 | tf_op jit(solution)/shard_map/dot_general | solution.py:118
  398.3 5.0 %fusion.3 = bf16[1,208,6656]{2,1,0:T(8,128)(2,1)} fusion(f32[208,6656]{1,0:T(8,128)} %get-tuple-element.79, bf16[1,208,6656]{2,1,0:T(8,128)(2,1)S(1)} %copy-done.2, f32[6656]{0:T(1024)S(1)} %get-tuple-element.48, f32[208]{0:T(256)S(1)} %sqrt_multiply_fusion), kind=kLoop, calls=%fused_computation.11 | loop fusion | flops 6922240 | bytes 11103040 | tf_op jit(solution)/shard_map/broadcast_in_dim | solution.py:154
  (164 shorter events, 95.2 us)
Async XLA Ops:
  7.2 153.8 %all-gather.5.cloned.1.call-start = ((), (), s32[]{:S(2)}) async-start(), calls=%async_computation | async-start | bytes 7028736 | tf_op jit(solution)/shard_map/all_gather | solution.py:117
  8.2 6.5 %collective-permute-start.2 = (bf16[208,128]{1,0:T(8,128)(2,1)S(1)}, bf16[208,128]{1,0:T(8,128)(2,1)S(1)}, u32[]{:S(2)}, u32[]{:S(2)}) collective-permute-start(bf16[208,128]{1,0:T(8,128)(2,1)S(1)} %dynamic-slice_bitcast_fusion), channel_id=1, source_target_pairs={{0,2},{2,4},{4,6},{6,0},{1,3},{3,5},{5,7},{7,1},{8,10},{10,12},{12... | collective-permute-start | bytes 159752 | tf_op jit(solution)/shard_map/ppermute | solution.py:15
  10.1 6.3 %collective-permute-start.1 = (bf16[208,128]{1,0:T(8,128)(2,1)S(1)}, bf16[208,128]{1,0:T(8,128)(2,1)S(1)}, u32[]{:S(2)}, u32[]{:S(2)}) collective-permute-start(bf16[208,128]{1,0:T(8,128)(2,1)S(1)} %dynamic-slice_bitcast_fusion), channel_id=1, source_target_pairs={{0,4},{2,6},{4,0},{6,2},{1,5},{3,7},{5,1},{7,3},{8,12},{10,14},{12... | collective-permute-start | bytes 159752 | tf_op jit(solution)/shard_map/ppermute | solution.py:15
  20.1 8.9 %collective-permute-start.5 = (bf16[4,208,128]{2,1,0:T(8,128)(2,1)}, bf16[4,208,128]{2,1,0:T(8,128)(2,1)S(1)}, u32[]{:S(2)}, u32[]{:S(2)}) collective-permute-start(bf16[4,208,128]{2,1,0:T(8,128)(2,1)} %pad_maximum_fusion.2), channel_id=1, source_target_pairs={{0,8},{8,16},{16,24},{24,0},{1,9},{9,17},{17,25},{25,1},{2,10},{10... | collective-permute-start | bytes 638984 | tf_op jit(solution)/shard_map/ppermute | solution.py:15
  21.7 11.2 %collective-permute-start.4 = (bf16[4,208,128]{2,1,0:T(8,128)(2,1)}, bf16[4,208,128]{2,1,0:T(8,128)(2,1)S(1)}, u32[]{:S(2)}, u32[]{:S(2)}) collective-permute-start(bf16[4,208,128]{2,1,0:T(8,128)(2,1)} %pad_maximum_fusion.2), channel_id=1, source_target_pairs={{0,16},{8,24},{16,0},{24,8},{1,17},{9,25},{17,1},{25,9},{2,18},{10... | collective-permute-start | bytes 638984 | tf_op jit(solution)/shard_map/ppermute | solution.py:15
  24.6 8.3 %collective-permute-start.3 = (bf16[4,208,128]{2,1,0:T(8,128)(2,1)}, bf16[4,208,128]{2,1,0:T(8,128)(2,1)S(1)}, u32[]{:S(2)}, u32[]{:S(2)}) collective-permute-start(bf16[4,208,128]{2,1,0:T(8,128)(2,1)} %pad_maximum_fusion.2), channel_id=1, source_target_pairs={{0,24},{8,0},{16,8},{24,16},{1,25},{9,1},{17,9},{25,17},{2,26},{10... | collective-permute-start | bytes 638984 | tf_op jit(solution)/shard_map/ppermute | solution.py:15
  59.6 11.0 %collective-permute-start.13 = (f32[3,128]{1,0:T(4,128)S(1)}, f32[3,128]{1,0:T(4,128)S(1)}, u32[]{:S(2)}, u32[]{:S(2)}) collective-permute-start(f32[3,128]{1,0:T(4,128)S(1)} %add_add_fusion.3), channel_id=1, source_target_pairs={{0,8},{8,16},{16,24},{24,0},{1,9},{9,17},{17,25},{25,1},{2,10},{10... | collective-permute-start | bytes 4616 | tf_op jit(solution)/shard_map/ppermute | solution.py:15
  60.1 10.5 %collective-permute-start.12 = (f32[3,128]{1,0:T(4,128)S(1)}, f32[3,128]{1,0:T(4,128)S(1)}, u32[]{:S(2)}, u32[]{:S(2)}) collective-permute-start(f32[3,128]{1,0:T(4,128)S(1)} %add_add_fusion.3), channel_id=1, source_target_pairs={{0,24},{8,0},{16,8},{24,16},{1,25},{9,1},{17,9},{25,17},{2,26},{10... | collective-permute-start | bytes 4616 | tf_op jit(solution)/shard_map/ppermute | solution.py:15
  62.9 7.8 %collective-permute-start.11 = (f32[3,128]{1,0:T(4,128)S(1)}, f32[3,128]{1,0:T(4,128)S(1)}, u32[]{:S(2)}, u32[]{:S(2)}) collective-permute-start(f32[3,128]{1,0:T(4,128)S(1)} %add_add_fusion.3), channel_id=1, source_target_pairs={{0,16},{8,24},{16,0},{24,8},{1,17},{9,25},{17,1},{25,9},{2,18},{10... | collective-permute-start | bytes 4616 | tf_op jit(solution)/shard_map/ppermute | solution.py:15
  79.4 13.1 %collective-permute-start.18 = (bf16[4,208,128]{2,1,0:T(8,128)(2,1)S(1)}, bf16[4,208,128]{2,1,0:T(8,128)(2,1)S(1)}, u32[]{:S(2)}, u32[]{:S(2)}) collective-permute-start(bf16[4,208,128]{2,1,0:T(8,128)(2,1)S(1)} %get-tuple-element.50), channel_id=1, source_target_pairs={{0,8},{8,16},{16,24},{24,0},{1,9},{9,17},{17,25},{25,1},{2,10},{10... | collective-permute-start | bytes 638984 | tf_op jit(solution)/shard_map/ppermute | solution.py:59
  79.9 12.7 %collective-permute-start.20 = (bf16[4,208,128]{2,1,0:T(8,128)(2,1)S(1)}, bf16[4,208,128]{2,1,0:T(8,128)(2,1)S(1)}, u32[]{:S(2)}, u32[]{:S(2)}) collective-permute-start(bf16[4,208,128]{2,1,0:T(8,128)(2,1)S(1)} %get-tuple-element.51), channel_id=1, source_target_pairs={{0,24},{8,0},{16,8},{24,16},{1,25},{9,1},{17,9},{25,17},{2,26},{10... | collective-permute-start | bytes 638984 | tf_op jit(solution)/shard_map/ppermute | solution.py:59
  82.8 9.8 %collective-permute-start.19 = (bf16[4,208,128]{2,1,0:T(8,128)(2,1)S(1)}, bf16[4,208,128]{2,1,0:T(8,128)(2,1)S(1)}, u32[]{:S(2)}, u32[]{:S(2)}) collective-permute-start(bf16[4,208,128]{2,1,0:T(8,128)(2,1)S(1)} %get-tuple-element.52), channel_id=1, source_target_pairs={{0,16},{8,24},{16,0},{24,8},{1,17},{9,25},{17,1},{25,9},{2,18},{10... | collective-permute-start | bytes 638984 | tf_op jit(solution)/shard_map/ppermute | solution.py:59
  111.0 114.6 %all-gather.7.cloned.1.call-start = ((), (), s32[]{:S(2)}) async-start(), calls=%async_computation.1 | async-start | bytes 7028736 | tf_op jit(solution)/shard_map/all_gather | solution.py:117
  166.4 7.7 %collective-permute-start.27 = (bf16[208,512]{1,0:T(8,128)(2,1)S(1)}, bf16[208,512]{1,0:T(8,128)(2,1)S(1)}, u32[]{:S(2)}, u32[]{:S(2)}) collective-permute-start(bf16[208,512]{1,0:T(8,128)(2,1)S(1)} %fusion.27), channel_id=1, source_target_pairs={{32,0},{64,32},{96,64},{33,1},{65,33},{97,65},{34,2},{66,34},{98,6... | collective-permute-start | bytes 638984 | tf_op jit(solution)/shard_map/ppermute | solution.py:122
  174.8 114.4 %all-gather.9.cloned.1.call-start = ((), (), s32[]{:S(2)}) async-start(), calls=%async_computation.2 | async-start | bytes 7028736 | tf_op jit(solution)/shard_map/all_gather | solution.py:117
  230.1 7.7 %collective-permute-start.28 = (bf16[208,512]{1,0:T(8,128)(2,1)S(1)}, bf16[208,512]{1,0:T(8,128)(2,1)S(1)}, u32[]{:S(2)}, u32[]{:S(2)}) collective-permute-start(bf16[208,512]{1,0:T(8,128)(2,1)S(1)} %add_convert_fusion.2), channel_id=1, source_target_pairs={{32,0},{64,32},{96,64},{33,1},{65,33},{97,65},{34,2},{66,34},{98,6... | collective-permute-start | bytes 638984 | tf_op jit(solution)/shard_map/ppermute | solution.py:122
  238.5 114.4 %all-gather.11.cloned.1.call-start = ((), (), s32[]{:S(2)}) async-start(), calls=%async_computation.3 | async-start | bytes 7028736 | tf_op jit(solution)/shard_map/all_gather | solution.py:117
  293.8 7.7 %collective-permute-start.29 = (bf16[208,512]{1,0:T(8,128)(2,1)S(1)}, bf16[208,512]{1,0:T(8,128)(2,1)S(1)}, u32[]{:S(2)}, u32[]{:S(2)}) collective-permute-start(bf16[208,512]{1,0:T(8,128)(2,1)S(1)} %add_convert_fusion.1), channel_id=1, source_target_pairs={{32,0},{64,32},{96,64},{33,1},{65,33},{97,65},{34,2},{66,34},{98,6... | collective-permute-start | bytes 638984 | tf_op jit(solution)/shard_map/ppermute | solution.py:122
  360.5 24.9 %collective-permute-start.32 = (f32[105,128]{1,0:T(8,128)S(1)}, f32[105,128]{1,0:T(8,128)S(1)}, u32[]{:S(2)}, u32[]{:S(2)}) collective-permute-start(f32[105,128]{1,0:T(8,128)S(1)} %fusion.45), channel_id=1, source_target_pairs={{0,6},{2,0},{4,2},{6,4},{1,7},{3,1},{5,3},{7,5},{8,14},{10,8},{12,... | collective-permute-start | bytes 161288 | tf_op jit(solution)/shard_map/ppermute | solution.py:15
  362.4 23.0 %collective-permute-start.33 = (f32[105,128]{1,0:T(8,128)S(1)}, f32[105,128]{1,0:T(8,128)S(1)}, u32[]{:S(2)}, u32[]{:S(2)}) collective-permute-start(f32[105,128]{1,0:T(8,128)S(1)} %fusion.45), channel_id=1, source_target_pairs={{0,2},{2,4},{4,6},{6,0},{1,3},{3,5},{5,7},{7,1},{8,10},{10,12},{12... | collective-permute-start | bytes 161288 | tf_op jit(solution)/shard_map/ppermute | solution.py:15
  362.6 22.8 %collective-permute-start.31 = (f32[105,128]{1,0:T(8,128)S(1)}, f32[105,128]{1,0:T(8,128)S(1)}, u32[]{:S(2)}, u32[]{:S(2)}) collective-permute-start(f32[105,128]{1,0:T(8,128)S(1)} %fusion.45), channel_id=1, source_target_pairs={{0,4},{2,6},{4,0},{6,2},{1,5},{3,7},{5,1},{7,3},{8,12},{10,14},{12... | collective-permute-start | bytes 161288 | tf_op jit(solution)/shard_map/ppermute | solution.py:15
  365.8 14.8 %collective-permute-start.16 = (f32[1]{0:T(128)}, f32[1]{0:T(128)}, u32[]{:S(2)}, u32[]{:S(2)}) collective-permute-start(f32[1]{0:T(128)} %bitcast.19), channel_id=1, source_target_pairs={{0,32},{32,64},{64,96},{96,0},{1,33},{33,65},{65,97},{97,1},{2,34}... | collective-permute-start | bytes 20 | tf_op jit(solution)/shard_map/ppermute | solution.py:15
  385.5 8.9 %collective-permute-start.36 = (f32[105,128]{1,0:T(8,128)S(1)}, f32[105,128]{1,0:T(8,128)S(1)}, u32[]{:S(2)}, u32[]{:S(2)}) collective-permute-start(f32[105,128]{1,0:T(8,128)S(1)} %add_add_fusion.1), channel_id=1, source_target_pairs={{0,8},{8,16},{16,24},{24,0},{1,9},{9,17},{17,25},{25,1},{2,10},{10... | collective-permute-start | bytes 161288 | tf_op jit(solution)/shard_map/ppermute | solution.py:15
  385.7 8.7 %collective-permute-start.35 = (f32[105,128]{1,0:T(8,128)S(1)}, f32[105,128]{1,0:T(8,128)S(1)}, u32[]{:S(2)}, u32[]{:S(2)}) collective-permute-start(f32[105,128]{1,0:T(8,128)S(1)} %add_add_fusion.1), channel_id=1, source_target_pairs={{0,24},{8,0},{16,8},{24,16},{1,25},{9,1},{17,9},{25,17},{2,26},{10... | collective-permute-start | bytes 161288 | tf_op jit(solution)/shard_map/ppermute | solution.py:15
  (39 other events, 539.9 us)
Sparse Core Ops, SparseCore 0:
  111.1 49.8 all-gather.4
  174.9 50.5 all-gather.6
  238.6 50.5 all-gather.8
  302.3 50.5 all-gather.10
where the time goes:
time: 412 us; the launch traced here: 411 us
  waiting for transfers between devices  252 us (61%)
  starting transfers between devices  58 us (14%)
  matrix products  42.8 us (10%)
  other arithmetic  25.7 us (6%)
  between operations  20 us (5%)
  local copies, waits for them, and re-layouts  11.9 us (3%)
    all_gather x4, waiting for transfers between devices, body(): full = lax.all_gather(dy, ('y', 'z', 'c'), axis=0, tiled=True)  194 us
    ppermute x27, starting transfers between devices, from_ring(): lax.ppermute(block, axis, [(i, (i - step) % size) for i in range(size)])  39.7 us
    ppermute x27, waiting for transfers between devices, from_ring(): lax.ppermute(block, axis, [(i, (i - step) % size) for i in range(size)])  28.8 us
    dot_general x4, matrix products, body(): backward = jnp.dot(local_weight, full, preferred_element_type=jnp.float32)  19.7 us
    ppermute x7, waiting for transfers between devices, scattered(): lax.ppermute(piece.astype(jnp.bfloat16), axis, [(i, (i + step) % size) fo...  14.8 us
    ppermute x3, waiting for transfers between devices, body(): dy = lax.ppermute(input_grad, 'x', [(i, i - 1) for i in range(1, 4)])  14.7 us
    ppermute x7, starting transfers between devices, scattered(): lax.ppermute(piece.astype(jnp.bfloat16), axis, [(i, (i + step) % size) fo...  9.77 us
    dot_general x1, matrix products, body(): lax.dot_general(head_weight, hidden_all, (((0,), (0,)), ((), ())), prefer...  8.39 us
  transfers between devices with their start and end apart: 41, of which 26 were waited for; matrix products, arithmetic and copies ran while one was open for 6% of the time, Pallas kernels for 0%

commit v1 on v0

--- a/solution.py
+++ b/solution.py
@@ -1,12 +1,23 @@
+import functools
 import jax
 import jax.numpy as jnp
 from jax import lax
 from jax.sharding import Mesh, PartitionSpec as P
+from jax.lax import all_to_all, axis_size
 
 decay_rate = 0.9
 learn_rate = 0.3
 tiny_term = 1e-30
 bf16_largest = 3.3895e38
+
+
+def answer_spans_now(u_in, chip_axis):
+    return jnp.concatenate(
+        all_to_all(jnp.stack(axis_size(chip_axis) * [u_in]), chip_axis, 0, 0), axis=0
+    )
+
+
+values_note = functools.partial(answer_spans_now, chip_axis=("y", "z", "c"))
 
 
 def from_ring(block, axis):
@@ -114,7 +125,7 @@
     gradient = jnp.zeros((rows_local, model_width), jnp.float32)
     for step in range(4):
         active = step == section_count - 1 - section_index
-        full = lax.all_gather(dy, ("y", "z", "c"), axis=0, tiled=True)
+        full = values_note(dy)
         backward = jnp.dot(local_weight, full, preferred_element_type=jnp.float32)
         input_grad = (dy.astype(jnp.float32) + backward).astype(jnp.bfloat16)
         outputs = jnp.where(active, input_grad, outputs)

time: 412 us -> 562 us (1.36); the launches traced: 411 us -> 554 us
  blocking collectives: 0 us -> 249 us
  waiting for transfers between devices: 252 us -> 141 us
  starting transfers between devices: 58 us -> 80.2 us
  between operations: 20 us -> 7.11 us
  matrix products: 42.8 us -> 33.2 us
  local copies, waits for them, and re-layouts: 11.9 us -> 19.2 us
    all_to_all x0 -> x3, blocking collectives: none -> 249 us  [answer_spans_now(): all_to_all(jnp.stack(axis_size(chip_axis) * [u_in]), chip_axis, 0, 0)]
    all_gather x4 -> x0, waiting for transfers between devices: 194 us -> none  [body(): full = lax.all_gather(dy, ('y', 'z', 'c'), axis=0, tiled=True)]
    all_to_all x0 -> x1, waiting for transfers between devices: none -> 80.6 us  [answer_spans_now(): all_to_all(jnp.stack(axis_size(chip_axis) * [u_in]), chip_axis, 0, 0)]
    ppermute x27, starting transfers between devices: 39.7 us -> 55.3 us  [from_ring(): lax.ppermute(block, axis, [(i, (i - step) % size) for i in range(size)])]
    dot_general x4, matrix products: 19.7 us -> 10.1 us  [body(): backward = jnp.dot(local_weight, full, preferred_element_type=jnp.float32)]
    another operation x0 -> x4, local copies, waits for them, and re-layouts: none -> 5.9 us  [answer_spans_now(): jnp.stack(axis_size(chip_axis) * [u_in])]
  transfers between devices with their start and end apart: 41 -> 38, of which waited for: 26 -> 22; matrix products, arithmetic and copies ran while one was open for 6% -> 4% of each run, Pallas kernels for 0% -> 0%
where the time goes in v1:
time: 562 us; the launch traced here: 554 us
  blocking collectives  249 us (44%)
  waiting for transfers between devices  141 us (25%)
  starting transfers between devices  80.2 us (14%)
  matrix products  33.2 us (6%)
  other arithmetic  25 us (4%)
  local copies, waits for them, and re-layouts  19.2 us (3%)
  between operations  7.11 us (1%)
    all_to_all x3, blocking collectives, answer_spans_now(): all_to_all(jnp.stack(axis_size(chip_axis) * [u_in]), chip_axis, 0, 0)  249 us
    all_to_all x1, waiting for transfers between devices, answer_spans_now(): all_to_all(jnp.stack(axis_size(chip_axis) * [u_in]), chip_axis, 0, 0)  80.6 us
    ppermute x27, starting transfers between devices, from_ring(): lax.ppermute(block, axis, [(i, (i - step) % size) for i in range(size)])  55.3 us
    ppermute x27, waiting for transfers between devices, from_ring(): lax.ppermute(block, axis, [(i, (i - step) % size) for i in range(size)])  29 us
    ppermute x3, waiting for transfers between devices, body(): dy = lax.ppermute(input_grad, 'x', [(i, i - 1) for i in range(1, 4)])  16.3 us
    ppermute x7, waiting for transfers between devices, scattered(): lax.ppermute(piece.astype(jnp.bfloat16), axis, [(i, (i + step) % size) fo...  14.8 us
  transfers between devices with their start and end apart: 38, of which 22 were waited for; matrix products, arithmetic and copies ran while one was open for 4% of the time, Pallas kernels for 0%

profile of v1, /device:TPU:6, one launch (start us, length us, event | category | flops | bytes accessed | tf_op | source)
XLA Modules:
  0.0 554.4 jit_solution(16432286730950697224)
XLA Ops:
  22.4 3.9 collective-permute-done.4
  35.9 8.4 %exponential_reduce_fusion = (f32[128]{0:T(128)S(1)}, f32[128]{0:T(128)S(1)}, bf16[1000,128]{1,0:T(8,128)(2,1)S(1)}) fusion(s32[1000]{0:T(1024)S(1)} %iota_add_fusion, s32[128]{0:T(128)S(1)} %dynamic_slice.7, bf16[6656,128]{1,0:T(8,128)(2,1)S(1)} %bitcast.261, bf16[6656,1000]{0,1:T(8,128)(2,1)} %param.17), kind=kOutput, calls=%fused_computation.43 | convolution fusion | flops 1704703744 | bytes 15277472 | tf_op jit(solution)/shard_map/dot_general | solution.py:94
  57.4 7.0 %convolution_bitcast_fusion = f32[6656,256]{0,1:T(8,128)S(1)} fusion(bf16[6656,1000]{0,1:T(8,128)(2,1)} %param.17, bf16[1000,128]{1,0:T(8,128)(2,1)S(1)} %compare_convert_fusion, bf16[1000,128]{1,0:T(8,128)(2,1)S(1)} %get-tuple-element.58), kind=kOutput, calls=%fused_computation | convolution fusion | flops 3408896000 | bytes 20639744 | tf_op jit(solution)/shard_map/dot_general | solution.py:115
  78.2 8.2 %collective-permute-done.18 = bf16[4,208,128]{2,1,0:T(8,128)(2,1)S(1)} collective-permute-done((bf16[4,208,128]{2,1,0:T(8,128)(2,1)S(1)}, bf16[4,208,128]{2,1,0:T(8,128)(2,1)S(1)}, u32[]{:S(2)}, u32[]{:S(2)}) %collective-permute-start.18) | collective-permute-done | bytes 213024 | tf_op jit(solution)/shard_map/ppermute | solution.py:70
  104.8 84.6 %all_to_all.20 = bf16[32,208,512]{2,1,0:T(8,128)(2,1)S(1)} all-to-all(bf16[32,208,512]{2,1,0:T(8,128)(2,1)S(1)} %stack.71), channel_id=1, replica_groups=mesh['x'=4,'y'=4,'z'=4,'c'=2] {'y','z','c'}, dimensions={0} | all-to-all | bytes 13631488 | tf_op jit(solution)/shard_map/all_to_all | solution.py:16
  193.5 5.6 %collective-permute-done.27 = bf16[208,512]{1,0:T(8,128)(2,1)S(1)} collective-permute-done((bf16[208,512]{1,0:T(8,128)(2,1)S(1)}, bf16[208,512]{1,0:T(8,128)(2,1)S(1)}, u32[]{:S(2)}, u32[]{:S(2)}) %collective-permute-start.27) | collective-permute-done | bytes 213024 | tf_op jit(solution)/shard_map/ppermute | solution.py:133
  199.9 82.0 %all_to_all.21 = bf16[32,208,512]{2,1,0:T(8,128)(2,1)S(1)} all-to-all(bf16[32,208,512]{2,1,0:T(8,128)(2,1)S(1)} %stack.72), channel_id=1, replica_groups=mesh['x'=4,'y'=4,'z'=4,'c'=2] {'y','z','c'}, dimensions={0} | all-to-all | bytes 13631488 | tf_op jit(solution)/shard_map/all_to_all | solution.py:16
  284.7 4.4 collective-permute-start.28
  289.1 5.4 collective-permute-done.28
  295.3 82.2 %all_to_all.22 = bf16[32,208,512]{2,1,0:T(8,128)(2,1)S(1)} all-to-all(bf16[32,208,512]{2,1,0:T(8,128)(2,1)S(1)} %stack.73), channel_id=1, replica_groups=mesh['x'=4,'y'=4,'z'=4,'c'=2] {'y','z','c'}, dimensions={0} | all-to-all | bytes 13631488 | tf_op jit(solution)/shard_map/all_to_all | solution.py:16
  380.2 4.4 collective-permute-start.29
  384.6 5.3 collective-permute-done.29
  390.0 3.6 stack.74
  393.6 5.0 all-to-all-start.3
  398.8 7.7 %conditional.4 = (f32[208,6656]{1,0:T(8,128)}) conditional(s32[]{:T(128)} %convert_element_type.126, () %tuple.32, (bf16[512,208]{1,0:T(8,128)(2,1)S(1)}, bf16[6656,512]{1,0:T(8,128)(2,1)}) %tuple.69), branch_computations={%region_4.5_spmd, %region_5.6_spmd} | conditional | flops 1417674752 | bytes 12566536 | solution.py:134
  398.8 7.7 %fusion.48 = f32[208,6656]{1,0:T(8,128)} fusion(bf16[512,208]{1,0:T(8,128)(2,1)S(1)} %get-tuple-element.28, bf16[6656,512]{1,0:T(8,128)(2,1)} %get-tuple-element.32), kind=kOutput, calls=%fused_computation.109 | convolution fusion | flops 1417674752 | bytes 12566528 | tf_op jit(solution)/shard_map/cond/branch_1_fun/dot_general | solution.py:136
  406.5 80.6 %all-to-all-done.3 = bf16[32,208,512]{2,1,0:T(8,128)(2,1)} async-done(((bf16[32,208,512]{2,1,0:T(8,128)(2,1)}), bf16[32,208,512]{2,1,0:T(8,128)(2,1)}, u32[]{:S(2)}, u32[]{:S(2)}) %all-to-all-start.3) | async-done | bytes 6815776 | tf_op jit(solution)/shard_map/all_to_all | solution.py:16
  494.7 7.9 %collective-permute-start.32 = (f32[105,128]{1,0:T(8,128)S(1)}, f32[105,128]{1,0:T(8,128)S(1)}, u32[]{:S(2)}, u32[]{:S(2)}) collective-permute-start(f32[105,128]{1,0:T(8,128)S(1)} %fusion.45), channel_id=1, source_target_pairs={{0,6},{2,0},{4,2},{6,4},{1,7},{3,1},{5,3},{7,5},{8,14},{10,8},{12,... | collective-permute-start | bytes 161288 | tf_op jit(solution)/shard_map/ppermute | solution.py:26
  502.7 4.3 collective-permute-start.33
  510.1 11.1 %collective-permute-start.16 = (f32[1]{0:T(128)}, f32[1]{0:T(128)}, u32[]{:S(2)}, u32[]{:S(2)}) collective-permute-start(f32[1]{0:T(128)} %bitcast.19), channel_id=1, source_target_pairs={{0,32},{32,64},{64,96},{96,0},{1,33},{33,65},{65,97},{97,1},{2,34}... | collective-permute-start | bytes 20 | tf_op jit(solution)/shard_map/ppermute | solution.py:26
  521.9 4.6 collective-permute-done.14
  527.8 3.7 collective-permute-done.15
  538.9 5.2 fusion.36
  548.0 5.0 fusion.3
  (159 shorter events, 107.0 us)
Async XLA Ops:
  1.6 6.5 %collective-permute-start.2 = (bf16[208,128]{1,0:T(8,128)(2,1)S(1)}, bf16[208,128]{1,0:T(8,128)(2,1)S(1)}, u32[]{:S(2)}, u32[]{:S(2)}) collective-permute-start(bf16[208,128]{1,0:T(8,128)(2,1)S(1)} %dynamic-slice_bitcast_fusion), channel_id=1, source_target_pairs={{0,2},{2,4},{4,6},{6,0},{1,3},{3,5},{5,7},{7,1},{8,10},{10,12},{12... | collective-permute-start | bytes 159752 | tf_op jit(solution)/shard_map/ppermute | solution.py:26
  3.5 6.3 %collective-permute-start.1 = (bf16[208,128]{1,0:T(8,128)(2,1)S(1)}, bf16[208,128]{1,0:T(8,128)(2,1)S(1)}, u32[]{:S(2)}, u32[]{:S(2)}) collective-permute-start(bf16[208,128]{1,0:T(8,128)(2,1)S(1)} %dynamic-slice_bitcast_fusion), channel_id=1, source_target_pairs={{0,4},{2,6},{4,0},{6,2},{1,5},{3,7},{5,1},{7,3},{8,12},{10,14},{12... | collective-permute-start | bytes 159752 | tf_op jit(solution)/shard_map/ppermute | solution.py:26
  13.5 8.9 %collective-permute-start.5 = (bf16[4,208,128]{2,1,0:T(8,128)(2,1)}, bf16[4,208,128]{2,1,0:T(8,128)(2,1)S(1)}, u32[]{:S(2)}, u32[]{:S(2)}) collective-permute-start(bf16[4,208,128]{2,1,0:T(8,128)(2,1)} %pad_maximum_fusion.2), channel_id=1, source_target_pairs={{0,8},{8,16},{16,24},{24,0},{1,9},{9,17},{17,25},{25,1},{2,10},{10... | collective-permute-start | bytes 638984 | tf_op jit(solution)/shard_map/ppermute | solution.py:26
  15.1 11.2 %collective-permute-start.4 = (bf16[4,208,128]{2,1,0:T(8,128)(2,1)}, bf16[4,208,128]{2,1,0:T(8,128)(2,1)S(1)}, u32[]{:S(2)}, u32[]{:S(2)}) collective-permute-start(bf16[4,208,128]{2,1,0:T(8,128)(2,1)} %pad_maximum_fusion.2), channel_id=1, source_target_pairs={{0,16},{8,24},{16,0},{24,8},{1,17},{9,25},{17,1},{25,9},{2,18},{10... | collective-permute-start | bytes 638984 | tf_op jit(solution)/shard_map/ppermute | solution.py:26
  18.0 8.3 %collective-permute-start.3 = (bf16[4,208,128]{2,1,0:T(8,128)(2,1)}, bf16[4,208,128]{2,1,0:T(8,128)(2,1)S(1)}, u32[]{:S(2)}, u32[]{:S(2)}) collective-permute-start(bf16[4,208,128]{2,1,0:T(8,128)(2,1)} %pad_maximum_fusion.2), channel_id=1, source_target_pairs={{0,24},{8,0},{16,8},{24,16},{1,25},{9,1},{17,9},{25,17},{2,26},{10... | collective-permute-start | bytes 638984 | tf_op jit(solution)/shard_map/ppermute | solution.py:26
  53.0 11.4 %collective-permute-start.13 = (f32[3,128]{1,0:T(4,128)S(1)}, f32[3,128]{1,0:T(4,128)S(1)}, u32[]{:S(2)}, u32[]{:S(2)}) collective-permute-start(f32[3,128]{1,0:T(4,128)S(1)} %add_add_fusion.3), channel_id=1, source_target_pairs={{0,8},{8,16},{16,24},{24,0},{1,9},{9,17},{17,25},{25,1},{2,10},{10... | collective-permute-start | bytes 4616 | tf_op jit(solution)/shard_map/ppermute | solution.py:26
  53.5 10.9 %collective-permute-start.12 = (f32[3,128]{1,0:T(4,128)S(1)}, f32[3,128]{1,0:T(4,128)S(1)}, u32[]{:S(2)}, u32[]{:S(2)}) collective-permute-start(f32[3,128]{1,0:T(4,128)S(1)} %add_add_fusion.3), channel_id=1, source_target_pairs={{0,24},{8,0},{16,8},{24,16},{1,25},{9,1},{17,9},{25,17},{2,26},{10... | collective-permute-start | bytes 4616 | tf_op jit(solution)/shard_map/ppermute | solution.py:26
  56.3 8.1 %collective-permute-start.11 = (f32[3,128]{1,0:T(4,128)S(1)}, f32[3,128]{1,0:T(4,128)S(1)}, u32[]{:S(2)}, u32[]{:S(2)}) collective-permute-start(f32[3,128]{1,0:T(4,128)S(1)} %add_add_fusion.3), channel_id=1, source_target_pairs={{0,16},{8,24},{16,0},{24,8},{1,17},{9,25},{17,1},{25,9},{2,18},{10... | collective-permute-start | bytes 4616 | tf_op jit(solution)/shard_map/ppermute | solution.py:26
  73.2 13.1 %collective-permute-start.18 = (bf16[4,208,128]{2,1,0:T(8,128)(2,1)S(1)}, bf16[4,208,128]{2,1,0:T(8,128)(2,1)S(1)}, u32[]{:S(2)}, u32[]{:S(2)}) collective-permute-start(bf16[4,208,128]{2,1,0:T(8,128)(2,1)S(1)} %get-tuple-element.50), channel_id=1, source_target_pairs={{0,8},{8,16},{16,24},{24,0},{1,9},{9,17},{17,25},{25,1},{2,10},{10... | collective-permute-start | bytes 638984 | tf_op jit(solution)/shard_map/ppermute | solution.py:70
  73.6 12.7 %collective-permute-start.20 = (bf16[4,208,128]{2,1,0:T(8,128)(2,1)S(1)}, bf16[4,208,128]{2,1,0:T(8,128)(2,1)S(1)}, u32[]{:S(2)}, u32[]{:S(2)}) collective-permute-start(bf16[4,208,128]{2,1,0:T(8,128)(2,1)S(1)} %get-tuple-element.51), channel_id=1, source_target_pairs={{0,24},{8,0},{16,8},{24,16},{1,25},{9,1},{17,9},{25,17},{2,26},{10... | collective-permute-start | bytes 638984 | tf_op jit(solution)/shard_map/ppermute | solution.py:70
  76.5 9.8 %collective-permute-start.19 = (bf16[4,208,128]{2,1,0:T(8,128)(2,1)S(1)}, bf16[4,208,128]{2,1,0:T(8,128)(2,1)S(1)}, u32[]{:S(2)}, u32[]{:S(2)}) collective-permute-start(bf16[4,208,128]{2,1,0:T(8,128)(2,1)S(1)} %get-tuple-element.52), channel_id=1, source_target_pairs={{0,16},{8,24},{16,0},{24,8},{1,17},{9,25},{17,1},{25,9},{2,18},{10... | collective-permute-start | bytes 638984 | tf_op jit(solution)/shard_map/ppermute | solution.py:70
  89.9 5.6 %collective-permute-start.22 = (bf16[208,128]{1,0:T(8,128)(2,1)S(1)}, bf16[208,128]{1,0:T(8,128)(2,1)S(1)}, u32[]{:S(2)}, u32[]{:S(2)}) collective-permute-start(bf16[208,128]{1,0:T(8,128)(2,1)S(1)} %get-tuple-element.61), channel_id=1, source_target_pairs={{0,4},{2,6},{4,0},{6,2},{1,5},{3,7},{5,1},{7,3},{8,12},{10,14},{12... | collective-permute-start | bytes 159752 | tf_op jit(solution)/shard_map/ppermute | solution.py:70
  96.2 5.6 %collective-permute-start.25 = (bf16[208,128]{1,0:T(8,128)(2,1)S(1)}, bf16[208,128]{1,0:T(8,128)(2,1)S(1)}, u32[]{:S(2)}, u32[]{:S(2)}) collective-permute-start(bf16[208,128]{1,0:T(8,128)(2,1)S(1)} %add_convert_fusion.3), channel_id=1, source_target_pairs={{0,64},{32,96},{64,0},{96,32},{1,65},{33,97},{65,1},{97,33},{2,66}... | collective-permute-start | bytes 159752 | tf_op jit(solution)/shard_map/ppermute | solution.py:26
  192.2 6.9 %collective-permute-start.27 = (bf16[208,512]{1,0:T(8,128)(2,1)S(1)}, bf16[208,512]{1,0:T(8,128)(2,1)S(1)}, u32[]{:S(2)}, u32[]{:S(2)}) collective-permute-start(bf16[208,512]{1,0:T(8,128)(2,1)S(1)} %fusion.27), channel_id=1, source_target_pairs={{32,0},{64,32},{96,64},{33,1},{65,33},{97,65},{34,2},{66,34},{98,6... | collective-permute-start | bytes 638984 | tf_op jit(solution)/shard_map/ppermute | solution.py:133
  284.7 9.8 %collective-permute-start.28 = (bf16[208,512]{1,0:T(8,128)(2,1)S(1)}, bf16[208,512]{1,0:T(8,128)(2,1)S(1)}, u32[]{:S(2)}, u32[]{:S(2)}) collective-permute-start(bf16[208,512]{1,0:T(8,128)(2,1)S(1)} %add_convert_fusion.2), channel_id=1, source_target_pairs={{32,0},{64,32},{96,64},{33,1},{65,33},{97,65},{34,2},{66,34},{98,6... | collective-permute-start | bytes 638984 | tf_op jit(solution)/shard_map/ppermute | solution.py:133
  380.2 9.7 %collective-permute-start.29 = (bf16[208,512]{1,0:T(8,128)(2,1)S(1)}, bf16[208,512]{1,0:T(8,128)(2,1)S(1)}, u32[]{:S(2)}, u32[]{:S(2)}) collective-permute-start(bf16[208,512]{1,0:T(8,128)(2,1)S(1)} %add_convert_fusion.1), channel_id=1, source_target_pairs={{32,0},{64,32},{96,64},{33,1},{65,33},{97,65},{34,2},{66,34},{98,6... | collective-permute-start | bytes 638984 | tf_op jit(solution)/shard_map/ppermute | solution.py:133
  393.6 93.6 %all-to-all-start.3 = ((bf16[32,208,512]{2,1,0:T(8,128)(2,1)}), bf16[32,208,512]{2,1,0:T(8,128)(2,1)}, u32[]{:S(2)}, u32[]{:S(2)}) async-start(bf16[32,208,512]{2,1,0:T(8,128)(2,1)} %stack.74), calls=%async_computation.3 | async-start | bytes 13631488 | tf_op jit(solution)/shard_map/all_to_all | solution.py:16
  494.7 38.0 %collective-permute-start.32 = (f32[105,128]{1,0:T(8,128)S(1)}, f32[105,128]{1,0:T(8,128)S(1)}, u32[]{:S(2)}, u32[]{:S(2)}) collective-permute-start(f32[105,128]{1,0:T(8,128)S(1)} %fusion.45), channel_id=1, source_target_pairs={{0,6},{2,0},{4,2},{6,4},{1,7},{3,1},{5,3},{7,5},{8,14},{10,8},{12,... | collective-permute-start | bytes 161288 | tf_op jit(solution)/shard_map/ppermute | solution.py:26
  502.7 30.1 %collective-permute-start.33 = (f32[105,128]{1,0:T(8,128)S(1)}, f32[105,128]{1,0:T(8,128)S(1)}, u32[]{:S(2)}, u32[]{:S(2)}) collective-permute-start(f32[105,128]{1,0:T(8,128)S(1)} %fusion.45), channel_id=1, source_target_pairs={{0,2},{2,4},{4,6},{6,0},{1,3},{3,5},{5,7},{7,1},{8,10},{10,12},{12... | collective-permute-start | bytes 161288 | tf_op jit(solution)/shard_map/ppermute | solution.py:26
  507.0 25.7 %collective-permute-start.31 = (f32[105,128]{1,0:T(8,128)S(1)}, f32[105,128]{1,0:T(8,128)S(1)}, u32[]{:S(2)}, u32[]{:S(2)}) collective-permute-start(f32[105,128]{1,0:T(8,128)S(1)} %fusion.45), channel_id=1, source_target_pairs={{0,4},{2,6},{4,0},{6,2},{1,5},{3,7},{5,1},{7,3},{8,12},{10,14},{12... | collective-permute-start | bytes 161288 | tf_op jit(solution)/shard_map/ppermute | solution.py:26
  510.1 17.7 %collective-permute-start.16 = (f32[1]{0:T(128)}, f32[1]{0:T(128)}, u32[]{:S(2)}, u32[]{:S(2)}) collective-permute-start(f32[1]{0:T(128)} %bitcast.19), channel_id=1, source_target_pairs={{0,32},{32,64},{64,96},{96,0},{1,33},{33,65},{65,97},{97,1},{2,34}... | collective-permute-start | bytes 20 | tf_op jit(solution)/shard_map/ppermute | solution.py:26
  532.8 11.3 %collective-permute-start.36 = (f32[105,128]{1,0:T(8,128)S(1)}, f32[105,128]{1,0:T(8,128)S(1)}, u32[]{:S(2)}, u32[]{:S(2)}) collective-permute-start(f32[105,128]{1,0:T(8,128)S(1)} %add_add_fusion.1), channel_id=1, source_target_pairs={{0,8},{8,16},{16,24},{24,0},{1,9},{9,17},{17,25},{25,1},{2,10},{10... | collective-permute-start | bytes 161288 | tf_op jit(solution)/shard_map/ppermute | solution.py:26
  532.9 11.2 %collective-permute-start.35 = (f32[105,128]{1,0:T(8,128)S(1)}, f32[105,128]{1,0:T(8,128)S(1)}, u32[]{:S(2)}, u32[]{:S(2)}) collective-permute-start(f32[105,128]{1,0:T(8,128)S(1)} %add_add_fusion.1), channel_id=1, source_target_pairs={{0,24},{8,0},{16,8},{24,16},{1,25},{9,1},{17,9},{25,17},{2,26},{10... | collective-permute-start | bytes 161288 | tf_op jit(solution)/shard_map/ppermute | solution.py:26
  536.1 8.0 %collective-permute-start.34 = (f32[105,128]{1,0:T(8,128)S(1)}, f32[105,128]{1,0:T(8,128)S(1)}, u32[]{:S(2)}, u32[]{:S(2)}) collective-permute-start(f32[105,128]{1,0:T(8,128)S(1)} %add_add_fusion.1), channel_id=1, source_target_pairs={{0,16},{8,24},{16,0},{24,8},{1,17},{9,25},{17,1},{25,9},{2,18},{10... | collective-permute-start | bytes 161288 | tf_op jit(solution)/shard_map/ppermute | solution.py:26
  (35 other events, 558.9 us)
